TPU v7x, 32 devices: a whole 2x2x4 slice. The times are simulated.
32 devices in a mesh: level: 8 (over y, x, core), row: 4 (over z).
Axes of the slice: x: 2, y: 2, z: 4, core: 2. Of those that a mesh axis runs over, the one named last changes fastest.
Arguments:
- right_side: float32 [64, 32, 128], P('level'), may hold values from -6 to 6
- inverses: float32 [64, 128, 128], P('level'), as said below
- blocks: float32 [64, 8, 128, 128], P('level', 'row'), may hold values from -0.125 to 0.125
- sources: int32 [64, 8], P('level', 'row'), may hold values from -1 to 55, as said below
Outputs:
- solved: float32 [64, 32, 128], P('level')
Inputs may be any that keep to these rules, and one draw needn't show every extreme that they name: `sources`: the supernodes form an elimination tree: every supernode below the top level has one parent on the next level, and every supernode above level 0 has exactly one child. The entries of supernode t are its 8 highest-numbered descendants in that tree, distinct and in falling order, followed by -1 for empty slots; the supernodes of level 0 have only empty slots. `inverses`: lower triangular.
All inputs are finite; a program needn't handle non-finite values.
Results may differ from a plain program's by a relative error of at most 0.0001.
Values sent between devices are 32-bit elements; how exact they have to be, the bound alone decides.
No kernel may reach another device: no remote copies, remote signals or barrier semaphores. Data moves between devices by JAX's collectives and lax.ppermute only.
A program may use at most 64 MiB of HBM per device.

v0:
```python
import jax
import jax.numpy as jnp
from jax import lax
from jax.sharding import PartitionSpec as P


def spread(value, axis, source):
    kept = jnp.where(lax.axis_index(axis) == source, value, 0).astype(value.dtype)
    return lax.psum(kept, axis)


def per_device(right_side, inverses, blocks, sources):
    highest = lax.Precision.HIGHEST
    sn_count = right_side.shape[0]
    my_level = lax.axis_index("level")
    levels = lax.axis_size("level")

    def advance(level_now, carry):
        updates, solved = carry
        mine = my_level == level_now
        totals = lax.psum(updates, "row")
        own = jnp.einsum("snw,svw->snv", right_side - totals, inverses, precision=highest)
        current = spread(own, "level", level_now)
        solved = jnp.where(mine, current, solved)
        wanted = level_now * sn_count + jnp.arange(sn_count, dtype=jnp.int32)
        select = (sources[:, :, None] == wanted[None, None, :]).astype(jnp.float32)
        picked = jnp.einsum("srk,knw->srnw", select, current, precision=highest)
        updates = updates + jnp.einsum("srnw,srwv->snv", picked, blocks, precision=highest)
        return (updates, solved)

    empty = jnp.zeros(right_side.shape, jnp.float32)
    updates, solved = lax.fori_loop(0, levels, advance, (empty, empty))
    return solved


def solution(mesh):
    return jax.shard_map(
        per_device,
        mesh=mesh,
        in_specs=(
            P("level", None, None),
            P("level", None, None),
            P("level", "row", None, None),
            P("level", "row"),
        ),
        out_specs=P("level", None, None),
        check_vma=False,
    )
```

profile of v0, /device:TPU:0, one launch (start us, length us, event | category | flops | bytes accessed | tf_op | source)
XLA Modules:
  0.0 781.4 jit_solution(18321583379033328239)
XLA Ops:
  6.5 0.7 copy-done.4
  7.2 766.9 %while.18 = (s32[]{:T(128)}, f32[8,32,128]{2,1,0:T(8,128)S(1)}, f32[8,32,128]{2,1,0:T(8,128)S(1)}, s32[8,2]{0,1:T(2,128)S(1)}, f32[8,32,128]{2,1,0:T(8,128)}, /*...) while((s32[]{:T(128)}, f32[8,32,128]{2,1,0:T(8,128)S(1)}, ...), condition=%wide.region_3.4_spmd.clone, body=%wide.region_0.3_spmd.clone.sunk | while | flops 157548688 | bytes 10355576 | solution.py:32
  7.2 0.7 broadcast_select_fusion.2
  8.0 0.1 copy.24
  8.1 39.7 %all-reduce.3.cloned.1.call-done = f32[8,32,128]{2,1,0:T(8,128)} async-done(((f32[8,32,128]{2,1,0:T(8,128)}), f32[8,32,128]{2,1,0:T(8,128)}) %all-reduce.3.cloned.1.call-update) | async-done | bytes 131088 | tf_op jit(solution)/shard_map/while/body/eval_jaxpr/psum | solution.py:21
  47.7 2.8 convolution_select_fusion.2
  50.6 53.3 %all-reduce.5.cloned.1.call-done = f32[8,32,128]{2,1,0:T(8,128)} async-done(((f32[8,32,128]{2,1,0:T(8,128)}), f32[8,32,128]{2,1,0:T(8,128)}) %all-reduce.5.cloned.1.call-update) | async-done | bytes 131088 | tf_op jit(solution)/shard_map/while/body/eval_jaxpr/psum | solution.py:9
  103.9 1.2 fusion.22
  105.2 0.7 fusion.23
  105.9 0.2 copy-done.2
  106.2 0.7 broadcast_select_fusion.2
  107.1 36.3 %all-reduce.3.cloned.1.call-done = f32[8,32,128]{2,1,0:T(8,128)} async-done(((f32[8,32,128]{2,1,0:T(8,128)}), f32[8,32,128]{2,1,0:T(8,128)}) %all-reduce.3.cloned.1.call-update) | async-done | bytes 131088 | tf_op jit(solution)/shard_map/while/body/eval_jaxpr/psum | solution.py:21
  143.4 2.8 convolution_select_fusion.2
  146.2 53.2 %all-reduce.5.cloned.1.call-done = f32[8,32,128]{2,1,0:T(8,128)} async-done(((f32[8,32,128]{2,1,0:T(8,128)}), f32[8,32,128]{2,1,0:T(8,128)}) %all-reduce.5.cloned.1.call-update) | async-done | bytes 131088 | tf_op jit(solution)/shard_map/while/body/eval_jaxpr/psum | solution.py:9
  199.4 1.2 fusion.22
  200.7 0.7 fusion.23
  201.4 0.2 copy-done.2
  201.7 0.7 broadcast_select_fusion.2
  202.5 0.1 copy.24
  202.6 36.0 %all-reduce.3.cloned.1.call-done = f32[8,32,128]{2,1,0:T(8,128)} async-done(((f32[8,32,128]{2,1,0:T(8,128)}), f32[8,32,128]{2,1,0:T(8,128)}) %all-reduce.3.cloned.1.call-update) | async-done | bytes 131088 | tf_op jit(solution)/shard_map/while/body/eval_jaxpr/psum | solution.py:21
  238.6 2.8 convolution_select_fusion.2
  241.4 53.2 %all-reduce.5.cloned.1.call-done = f32[8,32,128]{2,1,0:T(8,128)} async-done(((f32[8,32,128]{2,1,0:T(8,128)}), f32[8,32,128]{2,1,0:T(8,128)}) %all-reduce.5.cloned.1.call-update) | async-done | bytes 131088 | tf_op jit(solution)/shard_map/while/body/eval_jaxpr/psum | solution.py:9
  294.6 1.2 fusion.22
  295.9 0.7 fusion.23
  296.6 0.2 copy-done.2
  296.9 0.7 broadcast_select_fusion.2
  297.7 0.1 copy.24
  297.8 36.3 %all-reduce.3.cloned.1.call-done = f32[8,32,128]{2,1,0:T(8,128)} async-done(((f32[8,32,128]{2,1,0:T(8,128)}), f32[8,32,128]{2,1,0:T(8,128)}) %all-reduce.3.cloned.1.call-update) | async-done | bytes 131088 | tf_op jit(solution)/shard_map/while/body/eval_jaxpr/psum | solution.py:21
  334.1 2.8 convolution_select_fusion.2
  336.9 53.3 %all-reduce.5.cloned.1.call-done = f32[8,32,128]{2,1,0:T(8,128)} async-done(((f32[8,32,128]{2,1,0:T(8,128)}), f32[8,32,128]{2,1,0:T(8,128)}) %all-reduce.5.cloned.1.call-update) | async-done | bytes 131088 | tf_op jit(solution)/shard_map/while/body/eval_jaxpr/psum | solution.py:9
  390.3 1.2 fusion.22
  391.5 0.7 fusion.23
  392.2 0.2 copy-done.2
  392.6 0.7 broadcast_select_fusion.2
  393.3 0.1 copy.24
  393.4 36.3 %all-reduce.3.cloned.1.call-done = f32[8,32,128]{2,1,0:T(8,128)} async-done(((f32[8,32,128]{2,1,0:T(8,128)}), f32[8,32,128]{2,1,0:T(8,128)}) %all-reduce.3.cloned.1.call-update) | async-done | bytes 131088 | tf_op jit(solution)/shard_map/while/body/eval_jaxpr/psum | solution.py:21
  429.7 2.8 convolution_select_fusion.2
  432.5 53.2 %all-reduce.5.cloned.1.call-done = f32[8,32,128]{2,1,0:T(8,128)} async-done(((f32[8,32,128]{2,1,0:T(8,128)}), f32[8,32,128]{2,1,0:T(8,128)}) %all-reduce.5.cloned.1.call-update) | async-done | bytes 131088 | tf_op jit(solution)/shard_map/while/body/eval_jaxpr/psum | solution.py:9
  485.8 1.2 fusion.22
  487.0 0.7 fusion.23
  487.7 0.2 copy-done.2
  488.0 0.7 broadcast_select_fusion.2
  488.8 0.1 copy.24
  488.9 36.3 %all-reduce.3.cloned.1.call-done = f32[8,32,128]{2,1,0:T(8,128)} async-done(((f32[8,32,128]{2,1,0:T(8,128)}), f32[8,32,128]{2,1,0:T(8,128)}) %all-reduce.3.cloned.1.call-update) | async-done | bytes 131088 | tf_op jit(solution)/shard_map/while/body/eval_jaxpr/psum | solution.py:21
  525.2 2.8 convolution_select_fusion.2
  528.0 53.2 %all-reduce.5.cloned.1.call-done = f32[8,32,128]{2,1,0:T(8,128)} async-done(((f32[8,32,128]{2,1,0:T(8,128)}), f32[8,32,128]{2,1,0:T(8,128)}) %all-reduce.5.cloned.1.call-update) | async-done | bytes 131088 | tf_op jit(solution)/shard_map/while/body/eval_jaxpr/psum | solution.py:9
  581.3 1.2 fusion.22
  582.5 0.7 fusion.23
  583.2 0.2 copy-done.2
  583.5 0.7 broadcast_select_fusion.2
  584.4 36.3 %all-reduce.3.cloned.1.call-done = f32[8,32,128]{2,1,0:T(8,128)} async-done(((f32[8,32,128]{2,1,0:T(8,128)}), f32[8,32,128]{2,1,0:T(8,128)}) %all-reduce.3.cloned.1.call-update) | async-done | bytes 131088 | tf_op jit(solution)/shard_map/while/body/eval_jaxpr/psum | solution.py:21
  620.7 2.8 convolution_select_fusion.2
  623.5 53.2 %all-reduce.5.cloned.1.call-done = f32[8,32,128]{2,1,0:T(8,128)} async-done(((f32[8,32,128]{2,1,0:T(8,128)}), f32[8,32,128]{2,1,0:T(8,128)}) %all-reduce.5.cloned.1.call-update) | async-done | bytes 131088 | tf_op jit(solution)/shard_map/while/body/eval_jaxpr/psum | solution.py:9
  676.8 1.2 fusion.22
  678.0 0.7 fusion.23
  678.7 0.2 copy-done.2
  679.1 0.7 broadcast_select_fusion.2
  679.9 36.0 %all-reduce.3.cloned.1.call-done = f32[8,32,128]{2,1,0:T(8,128)} async-done(((f32[8,32,128]{2,1,0:T(8,128)}), f32[8,32,128]{2,1,0:T(8,128)}) %all-reduce.3.cloned.1.call-update) | async-done | bytes 131088 | tf_op jit(solution)/shard_map/while/body/eval_jaxpr/psum | solution.py:21
  715.9 2.8 convolution_select_fusion.2
  718.7 53.2 %all-reduce.5.cloned.1.call-done = f32[8,32,128]{2,1,0:T(8,128)} async-done(((f32[8,32,128]{2,1,0:T(8,128)}), f32[8,32,128]{2,1,0:T(8,128)}) %all-reduce.5.cloned.1.call-update) | async-done | bytes 131088 | tf_op jit(solution)/shard_map/while/body/eval_jaxpr/psum | solution.py:9
  772.0 1.2 fusion.22
  773.2 0.7 fusion.23
  773.9 0.2 copy-done.2
  774.2 0.6 copy-done.3
  (103 shorter events, 2.2 us)
Async XLA Ops:
  6.5 0.7 copy-start.4
  7.2 98.0 %copy-start.1 = (f32[8,2,128,128]{3,2,1,0:T(8,128)S(1)}, f32[8,2,128,128]{3,2,1,0:T(8,128)}, u32[]{:S(2)}) copy-start(f32[8,2,128,128]{3,2,1,0:T(8,128)} %get-tuple-element.328) | copy-start | bytes 3145732 | tf_op jit(solution)/shard_map/while
  7.2 40.5 %all-reduce.3.cloned.1.call-start = ((), (), s32[]{:S(2)}) async-start(), calls=%async_computation | async-start | bytes 262144 | tf_op jit(solution)/shard_map/while/body/eval_jaxpr/psum | solution.py:21
  7.9 96.0 %all-reduce.5.cloned.1.call-start = ((), (), s32[]{:S(2)}) async-start(), calls=%async_computation.1 | async-start | bytes 262144 | tf_op jit(solution)/shard_map/while/body/eval_jaxpr/psum | solution.py:9
  103.9 1.2 copy-start
  105.2 0.9 copy-start.2
  106.2 94.5 %copy-start.1 = (f32[8,2,128,128]{3,2,1,0:T(8,128)S(1)}, f32[8,2,128,128]{3,2,1,0:T(8,128)}, u32[]{:S(2)}) copy-start(f32[8,2,128,128]{3,2,1,0:T(8,128)} %get-tuple-element.328) | copy-start | bytes 3145732 | tf_op jit(solution)/shard_map/while
  106.2 37.2 %all-reduce.3.cloned.1.call-start = ((), (), s32[]{:S(2)}) async-start(), calls=%async_computation | async-start | bytes 262144 | tf_op jit(solution)/shard_map/while/body/eval_jaxpr/psum | solution.py:21
  106.9 92.5 %all-reduce.5.cloned.1.call-start = ((), (), s32[]{:S(2)}) async-start(), calls=%async_computation.1 | async-start | bytes 262144 | tf_op jit(solution)/shard_map/while/body/eval_jaxpr/psum | solution.py:9
  199.4 1.2 copy-start
  200.7 0.9 copy-start.2
  201.7 94.2 %copy-start.1 = (f32[8,2,128,128]{3,2,1,0:T(8,128)S(1)}, f32[8,2,128,128]{3,2,1,0:T(8,128)}, u32[]{:S(2)}) copy-start(f32[8,2,128,128]{3,2,1,0:T(8,128)} %get-tuple-element.328) | copy-start | bytes 3145732 | tf_op jit(solution)/shard_map/while
  201.7 36.9 %all-reduce.3.cloned.1.call-start = ((), (), s32[]{:S(2)}) async-start(), calls=%async_computation | async-start | bytes 262144 | tf_op jit(solution)/shard_map/while/body/eval_jaxpr/psum | solution.py:21
  202.4 92.2 %all-reduce.5.cloned.1.call-start = ((), (), s32[]{:S(2)}) async-start(), calls=%async_computation.1 | async-start | bytes 262144 | tf_op jit(solution)/shard_map/while/body/eval_jaxpr/psum | solution.py:9
  294.6 1.2 copy-start
  295.9 0.9 copy-start.2
  296.9 94.7 %copy-start.1 = (f32[8,2,128,128]{3,2,1,0:T(8,128)S(1)}, f32[8,2,128,128]{3,2,1,0:T(8,128)}, u32[]{:S(2)}) copy-start(f32[8,2,128,128]{3,2,1,0:T(8,128)} %get-tuple-element.328) | copy-start | bytes 3145732 | tf_op jit(solution)/shard_map/while
  296.9 37.2 %all-reduce.3.cloned.1.call-start = ((), (), s32[]{:S(2)}) async-start(), calls=%async_computation | async-start | bytes 262144 | tf_op jit(solution)/shard_map/while/body/eval_jaxpr/psum | solution.py:21
  297.6 92.6 %all-reduce.5.cloned.1.call-start = ((), (), s32[]{:S(2)}) async-start(), calls=%async_computation.1 | async-start | bytes 262144 | tf_op jit(solution)/shard_map/while/body/eval_jaxpr/psum | solution.py:9
  390.3 1.2 copy-start
  391.5 0.9 copy-start.2
  392.5 94.5 %copy-start.1 = (f32[8,2,128,128]{3,2,1,0:T(8,128)S(1)}, f32[8,2,128,128]{3,2,1,0:T(8,128)}, u32[]{:S(2)}) copy-start(f32[8,2,128,128]{3,2,1,0:T(8,128)} %get-tuple-element.328) | copy-start | bytes 3145732 | tf_op jit(solution)/shard_map/while
  392.5 37.2 %all-reduce.3.cloned.1.call-start = ((), (), s32[]{:S(2)}) async-start(), calls=%async_computation | async-start | bytes 262144 | tf_op jit(solution)/shard_map/while/body/eval_jaxpr/psum | solution.py:21
  393.2 92.5 %all-reduce.5.cloned.1.call-start = ((), (), s32[]{:S(2)}) async-start(), calls=%async_computation.1 | async-start | bytes 262144 | tf_op jit(solution)/shard_map/while/body/eval_jaxpr/psum | solution.py:9
  485.8 1.2 copy-start
  487.0 0.9 copy-start.2
  488.0 94.5 %copy-start.1 = (f32[8,2,128,128]{3,2,1,0:T(8,128)S(1)}, f32[8,2,128,128]{3,2,1,0:T(8,128)}, u32[]{:S(2)}) copy-start(f32[8,2,128,128]{3,2,1,0:T(8,128)} %get-tuple-element.328) | copy-start | bytes 3145732 | tf_op jit(solution)/shard_map/while
  488.0 37.2 %all-reduce.3.cloned.1.call-start = ((), (), s32[]{:S(2)}) async-start(), calls=%async_computation | async-start | bytes 262144 | tf_op jit(solution)/shard_map/while/body/eval_jaxpr/psum | solution.py:21
  488.7 92.5 %all-reduce.5.cloned.1.call-start = ((), (), s32[]{:S(2)}) async-start(), calls=%async_computation.1 | async-start | bytes 262144 | tf_op jit(solution)/shard_map/while/body/eval_jaxpr/psum | solution.py:9
  581.3 1.2 copy-start
  582.5 0.9 copy-start.2
  583.5 94.5 %copy-start.1 = (f32[8,2,128,128]{3,2,1,0:T(8,128)S(1)}, f32[8,2,128,128]{3,2,1,0:T(8,128)}, u32[]{:S(2)}) copy-start(f32[8,2,128,128]{3,2,1,0:T(8,128)} %get-tuple-element.328) | copy-start | bytes 3145732 | tf_op jit(solution)/shard_map/while
  583.5 37.2 %all-reduce.3.cloned.1.call-start = ((), (), s32[]{:S(2)}) async-start(), calls=%async_computation | async-start | bytes 262144 | tf_op jit(solution)/shard_map/while/body/eval_jaxpr/psum | solution.py:21
  584.2 92.5 %all-reduce.5.cloned.1.call-start = ((), (), s32[]{:S(2)}) async-start(), calls=%async_computation.1 | async-start | bytes 262144 | tf_op jit(solution)/shard_map/while/body/eval_jaxpr/psum | solution.py:9
  676.8 1.2 copy-start
  678.0 0.9 copy-start.2
  679.0 94.2 %copy-start.1 = (f32[8,2,128,128]{3,2,1,0:T(8,128)S(1)}, f32[8,2,128,128]{3,2,1,0:T(8,128)}, u32[]{:S(2)}) copy-start(f32[8,2,128,128]{3,2,1,0:T(8,128)} %get-tuple-element.328) | copy-start | bytes 3145732 | tf_op jit(solution)/shard_map/while
  679.0 36.9 %all-reduce.3.cloned.1.call-start = ((), (), s32[]{:S(2)}) async-start(), calls=%async_computation | async-start | bytes 262144 | tf_op jit(solution)/shard_map/while/body/eval_jaxpr/psum | solution.py:21
  679.7 92.2 %all-reduce.5.cloned.1.call-start = ((), (), s32[]{:S(2)}) async-start(), calls=%async_computation.1 | async-start | bytes 262144 | tf_op jit(solution)/shard_map/while/body/eval_jaxpr/psum | solution.py:9
  772.0 1.2 copy-start
  773.2 0.9 copy-start.2
  774.2 0.7 copy-start.3
Sparse Core Ops, SparseCore 0:
  10.3 37.3 all-reduce.2
  50.8 53.1 all-reduce.4
  109.3 34.0 all-reduce.2
  146.3 53.1 all-reduce.4
  204.5 34.0 all-reduce.2
  241.5 53.1 all-reduce.4
  300.0 34.0 all-reduce.2
  337.1 53.1 all-reduce.4
  395.6 34.0 all-reduce.2
  432.6 53.1 all-reduce.4
  491.1 34.0 all-reduce.2
  528.1 53.1 all-reduce.4
  586.6 34.0 all-reduce.2
  623.6 53.1 all-reduce.4
  681.8 34.0 all-reduce.2
  718.8 53.1 all-reduce.4
where the time goes:
time: 782 us; the launch traced here: 781 us
  waiting for transfers between devices  719 us (92%)
  matrix products  37.5 us (5%)
  between operations  13.1 us (2%)
    psum x8, waiting for transfers between devices, spread(): return lax.psum(kept, axis)  426 us
    psum x8, waiting for transfers between devices, advance(): totals = lax.psum(updates, 'row')  293 us
    dot_general x8, matrix products, advance(): jnp.einsum('snw,svw->snv', right_side - totals, inverses, precision=highest)  22 us
  transfers between devices with their start and end apart: 16, of which 16 were waited for; matrix products, arithmetic and copies ran while one was open for 0% of the time, Pallas kernels for 0%

commit v1 on v0

--- a/solution.py
+++ b/solution.py
@@ -18,7 +18,7 @@
     def advance(level_now, carry):
         updates, solved = carry
         mine = my_level == level_now
-        totals = lax.psum(updates, "row")
+        totals = lax.all_gather(updates, axis_name="row").sum(axis=0)
         own = jnp.einsum("snw,svw->snv", right_side - totals, inverses, precision=highest)
         current = spread(own, "level", level_now)
         solved = jnp.where(mine, current, solved)

time: 782 us -> 602 us (0.77)
  waiting for transfers between devices: 719 us -> 432 us
  blocking collectives: 0 us -> 123 us
  matrix products: 37.5 us -> 28 us
    psum x8 -> x0, waiting for transfers between devices: 293 us -> none  [advance(): totals = lax.psum(updates, 'row')]
    all_gather x0 -> x8, blocking collectives: none -> 123 us  [advance(): totals = lax.all_gather(updates, axis_name='row').sum(axis=0)]
    dot_general x8, matrix products: 22 us -> 12.7 us  [advance(): jnp.einsum('snw,svw->snv', right_side - totals, inverses, precision=highest)]
  transfers between devices with their start and end apart: 16 -> 8, of which waited for: 16 -> 8; matrix products, arithmetic and copies ran while one was open for 0% -> 0% of each run, Pallas kernels for 0% -> 0%
where the time goes in v1:
time: 602 us; the launch traced here: 601 us
  waiting for transfers between devices  432 us (72%)
  blocking collectives  123 us (20%)
  matrix products  28 us (5%)
  between operations  13.4 us (2%)
    psum x8, waiting for transfers between devices, spread(): return lax.psum(kept, axis)  432 us
    all_gather x8, blocking collectives, advance(): totals = lax.all_gather(updates, axis_name='row').sum(axis=0)  123 us
    dot_general x8, matrix products, advance(): jnp.einsum('snw,svw->snv', right_side - totals, inverses, precision=highest)  12.7 us
  transfers between devices with their start and end apart: 8, of which 8 were waited for; matrix products, arithmetic and copies ran while one was open for 0% of the time, Pallas kernels for 0%

profile of v1, /device:TPU:0, one launch (start us, length us, event | category | flops | bytes accessed | tf_op | source)
XLA Modules:
  0.0 601.1 jit_solution(16876373846883631647)
XLA Ops:
  6.5 0.7 copy-done.5
  7.2 586.4 %while.18 = (s32[]{:T(128)}, f32[8,32,128]{2,1,0:T(8,128)S(1)}, f32[8,32,128]{2,1,0:T(8,128)S(1)}, s32[8,2]{0,1:T(2,128)S(1)}, f32[8,32,128]{2,1,0:T(8,128)}, /*...) while((s32[]{:T(128)}, f32[8,32,128]{2,1,0:T(8,128)S(1)}, ...), condition=%wide.region_3.4_spmd.clone, body=%wide.region_0.3_spmd.clone.sunk | while | flops 157614224 | bytes 12976624 | solution.py:32
  7.3 17.5 %all-gather.3 = f32[32,32,128]{2,1,0:T(8,128)S(1)} all-gather(f32[8,32,128]{2,1,0:T(8,128)S(1)} %broadcast_select_fusion.2), channel_id=2, replica_groups=mesh['level'=8,'row'=4] {'row'}, dimensions={0}, use_global_device_ids=true | all-gather | bytes 655360 | tf_op jit(solution)/shard_map/while/body/eval_jaxpr/all_gather | solution.py:21
  24.8 1.6 convolution_select_fusion.2
  26.4 0.0 all-reduce.2.cloned.1.call-update
  26.5 55.3 %all-reduce.2.cloned.1.call-done = f32[8,32,128]{2,1,0:T(8,128)} async-done(((f32[8,32,128]{2,1,0:T(8,128)}), f32[8,32,128]{2,1,0:T(8,128)}) %all-reduce.2.cloned.1.call-update) | async-done | bytes 131088 | tf_op jit(solution)/shard_map/while/body/eval_jaxpr/psum | solution.py:9
  81.8 1.2 fusion.26
  83.0 0.7 fusion.27
  83.7 0.2 copy-done.1
  84.0 0.0 all-reduce.2.cloned.1.call-start
  84.1 15.1 %all-gather.3 = f32[32,32,128]{2,1,0:T(8,128)S(1)} all-gather(f32[8,32,128]{2,1,0:T(8,128)S(1)} %broadcast_select_fusion.2), channel_id=2, replica_groups=mesh['level'=8,'row'=4] {'row'}, dimensions={0}, use_global_device_ids=true | all-gather | bytes 655360 | tf_op jit(solution)/shard_map/while/body/eval_jaxpr/all_gather | solution.py:21
  99.2 1.6 convolution_select_fusion.2
  100.8 0.0 all-reduce.2.cloned.1.call-update
  100.8 53.7 %all-reduce.2.cloned.1.call-done = f32[8,32,128]{2,1,0:T(8,128)} async-done(((f32[8,32,128]{2,1,0:T(8,128)}), f32[8,32,128]{2,1,0:T(8,128)}) %all-reduce.2.cloned.1.call-update) | async-done | bytes 131088 | tf_op jit(solution)/shard_map/while/body/eval_jaxpr/psum | solution.py:9
  154.6 1.2 fusion.26
  155.8 0.7 fusion.27
  156.5 0.2 copy-done.1
  156.8 0.0 all-reduce.2.cloned.1.call-start
  156.9 15.1 %all-gather.3 = f32[32,32,128]{2,1,0:T(8,128)S(1)} all-gather(f32[8,32,128]{2,1,0:T(8,128)S(1)} %broadcast_select_fusion.2), channel_id=2, replica_groups=mesh['level'=8,'row'=4] {'row'}, dimensions={0}, use_global_device_ids=true | all-gather | bytes 655360 | tf_op jit(solution)/shard_map/while/body/eval_jaxpr/all_gather | solution.py:21
  172.0 1.6 convolution_select_fusion.2
  173.6 0.0 all-reduce.2.cloned.1.call-update
  173.6 53.7 %all-reduce.2.cloned.1.call-done = f32[8,32,128]{2,1,0:T(8,128)} async-done(((f32[8,32,128]{2,1,0:T(8,128)}), f32[8,32,128]{2,1,0:T(8,128)}) %all-reduce.2.cloned.1.call-update) | async-done | bytes 131088 | tf_op jit(solution)/shard_map/while/body/eval_jaxpr/psum | solution.py:9
  227.4 1.2 fusion.26
  228.6 0.7 fusion.27
  229.3 0.2 copy-done.1
  229.6 0.0 all-reduce.2.cloned.1.call-start
  229.7 15.1 %all-gather.3 = f32[32,32,128]{2,1,0:T(8,128)S(1)} all-gather(f32[8,32,128]{2,1,0:T(8,128)S(1)} %broadcast_select_fusion.2), channel_id=2, replica_groups=mesh['level'=8,'row'=4] {'row'}, dimensions={0}, use_global_device_ids=true | all-gather | bytes 655360 | tf_op jit(solution)/shard_map/while/body/eval_jaxpr/all_gather | solution.py:21
  244.8 1.6 convolution_select_fusion.2
  246.4 0.0 all-reduce.2.cloned.1.call-update
  246.4 53.7 %all-reduce.2.cloned.1.call-done = f32[8,32,128]{2,1,0:T(8,128)} async-done(((f32[8,32,128]{2,1,0:T(8,128)}), f32[8,32,128]{2,1,0:T(8,128)}) %all-reduce.2.cloned.1.call-update) | async-done | bytes 131088 | tf_op jit(solution)/shard_map/while/body/eval_jaxpr/psum | solution.py:9
  300.2 1.2 fusion.26
  301.4 0.7 fusion.27
  302.1 0.2 copy-done.1
  302.4 0.0 all-reduce.2.cloned.1.call-start
  302.5 15.1 %all-gather.3 = f32[32,32,128]{2,1,0:T(8,128)S(1)} all-gather(f32[8,32,128]{2,1,0:T(8,128)S(1)} %broadcast_select_fusion.2), channel_id=2, replica_groups=mesh['level'=8,'row'=4] {'row'}, dimensions={0}, use_global_device_ids=true | all-gather | bytes 655360 | tf_op jit(solution)/shard_map/while/body/eval_jaxpr/all_gather | solution.py:21
  317.6 1.6 convolution_select_fusion.2
  319.2 0.0 all-reduce.2.cloned.1.call-update
  319.2 53.8 %all-reduce.2.cloned.1.call-done = f32[8,32,128]{2,1,0:T(8,128)} async-done(((f32[8,32,128]{2,1,0:T(8,128)}), f32[8,32,128]{2,1,0:T(8,128)}) %all-reduce.2.cloned.1.call-update) | async-done | bytes 131088 | tf_op jit(solution)/shard_map/while/body/eval_jaxpr/psum | solution.py:9
  373.0 1.2 fusion.26
  374.2 0.7 fusion.27
  374.9 0.2 copy-done.1
  375.2 0.0 all-reduce.2.cloned.1.call-start
  375.3 15.1 %all-gather.3 = f32[32,32,128]{2,1,0:T(8,128)S(1)} all-gather(f32[8,32,128]{2,1,0:T(8,128)S(1)} %broadcast_select_fusion.2), channel_id=2, replica_groups=mesh['level'=8,'row'=4] {'row'}, dimensions={0}, use_global_device_ids=true | all-gather | bytes 655360 | tf_op jit(solution)/shard_map/while/body/eval_jaxpr/all_gather | solution.py:21
  390.4 1.6 convolution_select_fusion.2
  392.1 53.7 %all-reduce.2.cloned.1.call-done = f32[8,32,128]{2,1,0:T(8,128)} async-done(((f32[8,32,128]{2,1,0:T(8,128)}), f32[8,32,128]{2,1,0:T(8,128)}) %all-reduce.2.cloned.1.call-update) | async-done | bytes 131088 | tf_op jit(solution)/shard_map/while/body/eval_jaxpr/psum | solution.py:9
  445.8 1.2 fusion.26
  447.0 0.7 fusion.27
  447.7 0.2 copy-done.1
  448.0 0.0 all-reduce.2.cloned.1.call-start
  448.1 15.1 %all-gather.3 = f32[32,32,128]{2,1,0:T(8,128)S(1)} all-gather(f32[8,32,128]{2,1,0:T(8,128)S(1)} %broadcast_select_fusion.2), channel_id=2, replica_groups=mesh['level'=8,'row'=4] {'row'}, dimensions={0}, use_global_device_ids=true | all-gather | bytes 655360 | tf_op jit(solution)/shard_map/while/body/eval_jaxpr/all_gather | solution.py:21
  463.2 1.6 convolution_select_fusion.2
  464.8 0.0 all-reduce.2.cloned.1.call-update
  464.8 53.8 %all-reduce.2.cloned.1.call-done = f32[8,32,128]{2,1,0:T(8,128)} async-done(((f32[8,32,128]{2,1,0:T(8,128)}), f32[8,32,128]{2,1,0:T(8,128)}) %all-reduce.2.cloned.1.call-update) | async-done | bytes 131088 | tf_op jit(solution)/shard_map/while/body/eval_jaxpr/psum | solution.py:9
  518.6 1.2 fusion.26
  519.8 0.7 fusion.27
  520.6 0.2 copy-done.1
  520.8 0.0 all-reduce.2.cloned.1.call-start
  520.9 15.1 %all-gather.3 = f32[32,32,128]{2,1,0:T(8,128)S(1)} all-gather(f32[8,32,128]{2,1,0:T(8,128)S(1)} %broadcast_select_fusion.2), channel_id=2, replica_groups=mesh['level'=8,'row'=4] {'row'}, dimensions={0}, use_global_device_ids=true | all-gather | bytes 655360 | tf_op jit(solution)/shard_map/while/body/eval_jaxpr/all_gather | solution.py:21
  536.0 1.6 convolution_select_fusion.2
  537.7 53.7 %all-reduce.2.cloned.1.call-done = f32[8,32,128]{2,1,0:T(8,128)} async-done(((f32[8,32,128]{2,1,0:T(8,128)}), f32[8,32,128]{2,1,0:T(8,128)}) %all-reduce.2.cloned.1.call-update) | async-done | bytes 131088 | tf_op jit(solution)/shard_map/while/body/eval_jaxpr/psum | solution.py:9
  591.4 1.2 fusion.26
  592.6 0.7 fusion.27
  593.4 0.2 copy-done.1
  593.6 0.6 copy-done.4
  (95 shorter events, 0.9 us)
Async XLA Ops:
  6.5 0.7 copy-start.5
  7.2 74.6 %all-reduce.2.cloned.1.call-start = ((), (), s32[]{:S(2)}) async-start(), calls=%async_computation | async-start | bytes 262144 | tf_op jit(solution)/shard_map/while/body/eval_jaxpr/psum | solution.py:9
  7.2 17.6 %copy-start.2 = (f32[8,128,128]{2,1,0:T(8,128)S(1)}, f32[8,128,128]{2,1,0:T(8,128)}, u32[]{:S(2)}) copy-start(f32[8,128,128]{2,1,0:T(8,128)} %get-tuple-element.329) | copy-start | bytes 1572868 | tf_op jit(solution)/shard_map/while
  7.2 17.6 %copy-start.3 = (f32[8,32,128]{2,1,0:T(8,128)S(1)}, f32[8,32,128]{2,1,0:T(8,128)}, u32[]{:S(2)}) copy-start(f32[8,32,128]{2,1,0:T(8,128)} %get-tuple-element.328) | copy-start | bytes 393220 | tf_op jit(solution)/shard_map/while
  24.8 58.2 %copy-start = (f32[8,2,128,128]{3,2,1,0:T(8,128)S(1)}, f32[8,2,128,128]{3,2,1,0:T(8,128)}, u32[]{:S(2)}) copy-start(f32[8,2,128,128]{3,2,1,0:T(8,128)} %get-tuple-element.330) | copy-start | bytes 3145732 | tf_op jit(solution)/shard_map/while
  83.0 0.9 copy-start.1
  84.0 70.6 %all-reduce.2.cloned.1.call-start = ((), (), s32[]{:S(2)}) async-start(), calls=%async_computation | async-start | bytes 262144 | tf_op jit(solution)/shard_map/while/body/eval_jaxpr/psum | solution.py:9
  84.1 15.1 %copy-start.2 = (f32[8,128,128]{2,1,0:T(8,128)S(1)}, f32[8,128,128]{2,1,0:T(8,128)}, u32[]{:S(2)}) copy-start(f32[8,128,128]{2,1,0:T(8,128)} %get-tuple-element.329) | copy-start | bytes 1572868 | tf_op jit(solution)/shard_map/while
  84.1 15.1 %copy-start.3 = (f32[8,32,128]{2,1,0:T(8,128)S(1)}, f32[8,32,128]{2,1,0:T(8,128)}, u32[]{:S(2)}) copy-start(f32[8,32,128]{2,1,0:T(8,128)} %get-tuple-element.328) | copy-start | bytes 393220 | tf_op jit(solution)/shard_map/while
  99.2 56.7 %copy-start = (f32[8,2,128,128]{3,2,1,0:T(8,128)S(1)}, f32[8,2,128,128]{3,2,1,0:T(8,128)}, u32[]{:S(2)}) copy-start(f32[8,2,128,128]{3,2,1,0:T(8,128)} %get-tuple-element.330) | copy-start | bytes 3145732 | tf_op jit(solution)/shard_map/while
  155.8 0.9 copy-start.1
  156.8 70.6 %all-reduce.2.cloned.1.call-start = ((), (), s32[]{:S(2)}) async-start(), calls=%async_computation | async-start | bytes 262144 | tf_op jit(solution)/shard_map/while/body/eval_jaxpr/psum | solution.py:9
  156.9 15.1 %copy-start.2 = (f32[8,128,128]{2,1,0:T(8,128)S(1)}, f32[8,128,128]{2,1,0:T(8,128)}, u32[]{:S(2)}) copy-start(f32[8,128,128]{2,1,0:T(8,128)} %get-tuple-element.329) | copy-start | bytes 1572868 | tf_op jit(solution)/shard_map/while
  156.9 15.1 %copy-start.3 = (f32[8,32,128]{2,1,0:T(8,128)S(1)}, f32[8,32,128]{2,1,0:T(8,128)}, u32[]{:S(2)}) copy-start(f32[8,32,128]{2,1,0:T(8,128)} %get-tuple-element.328) | copy-start | bytes 393220 | tf_op jit(solution)/shard_map/while
  171.9 56.7 %copy-start = (f32[8,2,128,128]{3,2,1,0:T(8,128)S(1)}, f32[8,2,128,128]{3,2,1,0:T(8,128)}, u32[]{:S(2)}) copy-start(f32[8,2,128,128]{3,2,1,0:T(8,128)} %get-tuple-element.330) | copy-start | bytes 3145732 | tf_op jit(solution)/shard_map/while
  228.6 0.9 copy-start.1
  229.6 70.6 %all-reduce.2.cloned.1.call-start = ((), (), s32[]{:S(2)}) async-start(), calls=%async_computation | async-start | bytes 262144 | tf_op jit(solution)/shard_map/while/body/eval_jaxpr/psum | solution.py:9
  229.7 15.1 %copy-start.2 = (f32[8,128,128]{2,1,0:T(8,128)S(1)}, f32[8,128,128]{2,1,0:T(8,128)}, u32[]{:S(2)}) copy-start(f32[8,128,128]{2,1,0:T(8,128)} %get-tuple-element.329) | copy-start | bytes 1572868 | tf_op jit(solution)/shard_map/while
  229.7 15.1 %copy-start.3 = (f32[8,32,128]{2,1,0:T(8,128)S(1)}, f32[8,32,128]{2,1,0:T(8,128)}, u32[]{:S(2)}) copy-start(f32[8,32,128]{2,1,0:T(8,128)} %get-tuple-element.328) | copy-start | bytes 393220 | tf_op jit(solution)/shard_map/while
  244.7 56.7 %copy-start = (f32[8,2,128,128]{3,2,1,0:T(8,128)S(1)}, f32[8,2,128,128]{3,2,1,0:T(8,128)}, u32[]{:S(2)}) copy-start(f32[8,2,128,128]{3,2,1,0:T(8,128)} %get-tuple-element.330) | copy-start | bytes 3145732 | tf_op jit(solution)/shard_map/while
  301.4 0.9 copy-start.1
  302.4 70.6 %all-reduce.2.cloned.1.call-start = ((), (), s32[]{:S(2)}) async-start(), calls=%async_computation | async-start | bytes 262144 | tf_op jit(solution)/shard_map/while/body/eval_jaxpr/psum | solution.py:9
  302.4 15.1 %copy-start.2 = (f32[8,128,128]{2,1,0:T(8,128)S(1)}, f32[8,128,128]{2,1,0:T(8,128)}, u32[]{:S(2)}) copy-start(f32[8,128,128]{2,1,0:T(8,128)} %get-tuple-element.329) | copy-start | bytes 1572868 | tf_op jit(solution)/shard_map/while
  302.5 15.1 %copy-start.3 = (f32[8,32,128]{2,1,0:T(8,128)S(1)}, f32[8,32,128]{2,1,0:T(8,128)}, u32[]{:S(2)}) copy-start(f32[8,32,128]{2,1,0:T(8,128)} %get-tuple-element.328) | copy-start | bytes 393220 | tf_op jit(solution)/shard_map/while
  317.5 56.7 %copy-start = (f32[8,2,128,128]{3,2,1,0:T(8,128)S(1)}, f32[8,2,128,128]{3,2,1,0:T(8,128)}, u32[]{:S(2)}) copy-start(f32[8,2,128,128]{3,2,1,0:T(8,128)} %get-tuple-element.330) | copy-start | bytes 3145732 | tf_op jit(solution)/shard_map/while
  374.2 0.9 copy-start.1
  375.2 70.6 %all-reduce.2.cloned.1.call-start = ((), (), s32[]{:S(2)}) async-start(), calls=%async_computation | async-start | bytes 262144 | tf_op jit(solution)/shard_map/while/body/eval_jaxpr/psum | solution.py:9
  375.3 15.1 %copy-start.2 = (f32[8,128,128]{2,1,0:T(8,128)S(1)}, f32[8,128,128]{2,1,0:T(8,128)}, u32[]{:S(2)}) copy-start(f32[8,128,128]{2,1,0:T(8,128)} %get-tuple-element.329) | copy-start | bytes 1572868 | tf_op jit(solution)/shard_map/while
  375.3 15.1 %copy-start.3 = (f32[8,32,128]{2,1,0:T(8,128)S(1)}, f32[8,32,128]{2,1,0:T(8,128)}, u32[]{:S(2)}) copy-start(f32[8,32,128]{2,1,0:T(8,128)} %get-tuple-element.328) | copy-start | bytes 393220 | tf_op jit(solution)/shard_map/while
  390.4 56.7 %copy-start = (f32[8,2,128,128]{3,2,1,0:T(8,128)S(1)}, f32[8,2,128,128]{3,2,1,0:T(8,128)}, u32[]{:S(2)}) copy-start(f32[8,2,128,128]{3,2,1,0:T(8,128)} %get-tuple-element.330) | copy-start | bytes 3145732 | tf_op jit(solution)/shard_map/while
  447.0 0.9 copy-start.1
  448.0 70.6 %all-reduce.2.cloned.1.call-start = ((), (), s32[]{:S(2)}) async-start(), calls=%async_computation | async-start | bytes 262144 | tf_op jit(solution)/shard_map/while/body/eval_jaxpr/psum | solution.py:9
  448.1 15.1 %copy-start.2 = (f32[8,128,128]{2,1,0:T(8,128)S(1)}, f32[8,128,128]{2,1,0:T(8,128)}, u32[]{:S(2)}) copy-start(f32[8,128,128]{2,1,0:T(8,128)} %get-tuple-element.329) | copy-start | bytes 1572868 | tf_op jit(solution)/shard_map/while
  448.1 15.1 %copy-start.3 = (f32[8,32,128]{2,1,0:T(8,128)S(1)}, f32[8,32,128]{2,1,0:T(8,128)}, u32[]{:S(2)}) copy-start(f32[8,32,128]{2,1,0:T(8,128)} %get-tuple-element.328) | copy-start | bytes 393220 | tf_op jit(solution)/shard_map/while
  463.2 56.7 %copy-start = (f32[8,2,128,128]{3,2,1,0:T(8,128)S(1)}, f32[8,2,128,128]{3,2,1,0:T(8,128)}, u32[]{:S(2)}) copy-start(f32[8,2,128,128]{3,2,1,0:T(8,128)} %get-tuple-element.330) | copy-start | bytes 3145732 | tf_op jit(solution)/shard_map/while
  519.8 0.9 copy-start.1
  520.8 70.6 %all-reduce.2.cloned.1.call-start = ((), (), s32[]{:S(2)}) async-start(), calls=%async_computation | async-start | bytes 262144 | tf_op jit(solution)/shard_map/while/body/eval_jaxpr/psum | solution.py:9
  520.9 15.1 %copy-start.2 = (f32[8,128,128]{2,1,0:T(8,128)S(1)}, f32[8,128,128]{2,1,0:T(8,128)}, u32[]{:S(2)}) copy-start(f32[8,128,128]{2,1,0:T(8,128)} %get-tuple-element.329) | copy-start | bytes 1572868 | tf_op jit(solution)/shard_map/while
  520.9 15.1 %copy-start.3 = (f32[8,32,128]{2,1,0:T(8,128)S(1)}, f32[8,32,128]{2,1,0:T(8,128)}, u32[]{:S(2)}) copy-start(f32[8,32,128]{2,1,0:T(8,128)} %get-tuple-element.328) | copy-start | bytes 393220 | tf_op jit(solution)/shard_map/while
  536.0 56.7 %copy-start = (f32[8,2,128,128]{3,2,1,0:T(8,128)S(1)}, f32[8,2,128,128]{3,2,1,0:T(8,128)}, u32[]{:S(2)}) copy-start(f32[8,2,128,128]{3,2,1,0:T(8,128)} %get-tuple-element.330) | copy-start | bytes 3145732 | tf_op jit(solution)/shard_map/while
  592.6 0.9 copy-start.1
  593.6 0.7 copy-start.4
Sparse Core Ops, SparseCore 0:
  26.6 55.1 all-reduce.1
  100.9 53.5 all-reduce.1
  173.7 53.5 all-reduce.1
  246.5 53.5 all-reduce.1
  319.3 53.6 all-reduce.1
  392.2 53.5 all-reduce.1
  464.9 53.6 all-reduce.1
  537.8 53.5 all-reduce.1
